TPU v7x, 32 devices: a whole 2x2x4 slice. The times are simulated.
32 devices in a mesh: row: 16 (over z, y, core), col: 2 (over x).
Axes of the slice: x: 2, y: 2, z: 4, core: 2. Of those that a mesh axis runs over, the one named last changes fastest.
Arguments:
- block_input: bfloat16 [25216, 768], P(('row', 'col')), may hold values from -60 to 60
- attention_in: bfloat16 [768, 2304], P('row', 'col'), may hold values from -0.21875 to 0.21875
- attention_out: bfloat16 [768, 768], P('row', 'col'), may hold values from -0.875 to 0.875
- expert_up: bfloat16 [16, 768, 3072], P('row', 'col'), may hold values from -0.21875 to 0.21875
- expert_down: bfloat16 [16, 3072, 768], P('row', None, 'col'), may hold values from -4 to 4
- router_weight: float32 [768, 16], replicated, may hold values from -0.109375 to 0.109375
- gain_attention: float32 [768], replicated, may hold values from 0.25 to 1.75
- gain_experts: float32 [768], replicated, may hold values from 0.25 to 1.75
- expert_ids: int32 [25216, 2], P(('row', 'col')), may hold values from 0 to 15, as said below
- expert_slots: int32 [25216, 2], P(('row', 'col')), may hold values from 0 to 135, as said below
- expert_capacity: int32 [16], replicated, may hold values from 68 to 136, as said below
- keep_mask: int32 [25216, 2], P(('row', 'col')), may hold values from 0 to 1
- output_grad: bfloat16 [25216, 768], P(('row', 'col')), may hold values from -6 to 6
Outputs:
- block_output: bfloat16 [25216, 768], P(('row', 'col'))
- input_grad: bfloat16 [25216, 768], P(('row', 'col'))
- attention_in_grad: float32 [768, 2304], P('row', 'col')
- attention_out_grad: float32 [768, 768], P('row', 'col')
- expert_up_grad: float32 [16, 768, 3072], P('row', 'col')
- expert_down_grad: float32 [16, 3072, 768], P('row', None, 'col')
- router_grad: float32 [768, 16], replicated
- gain_attention_grad: float32 [768], replicated
- gain_experts_grad: float32 [768], replicated
- residual_rms: float32 [3], replicated
Inputs may be any that keep to these rules, and one draw needn't show every extreme that they name: `expert_ids`: each row names two different experts. In each aligned block of 788 rows (the rows of one device) no expert is named more than 136 times and one expert is named exactly 136 times; blocks on the same index of col share that expert. `expert_slots`: within one aligned block of 788 rows, the n pairs that name one expert carry the slots 0 to n - 1, each once. `expert_capacity`: the expert named 136 times in the blocks of col index 0 accepts 136 slots.
All inputs are finite; a program needn't handle non-finite values.
Results may differ from a plain program's by a relative error of at most 0.019.
Values may be sent and summed in bfloat16 or wider, within the bound.
A program may use at most 192 MiB of HBM per device.

v0:
```python
import jax
import jax.numpy as jnp
from jax import lax
from jax.sharding import PartitionSpec as P

HEADS = 12
HEAD_DIM = 64
SEQ = 197
EXP_DEV = 1


epsilon = 1e-06
highest = lax.Precision.HIGHEST


def norm_rows(values, gain_vector):
    centred = values - jnp.mean(values, axis=-1, keepdims=True)
    inv_scale = lax.rsqrt(jnp.mean(centred * centred, axis=-1, keepdims=True) + epsilon)
    return centred * inv_scale * gain_vector


def gelu_exact(values):
    return 0.5 * values * (1.0 + lax.erf(values * 0.7071067811865476))


def route_gates(normed, router_weight, expert_ids):
    logits = jnp.dot(normed, router_weight, precision=highest)
    shifted = jnp.exp(logits - jnp.max(logits, axis=-1, keepdims=True))
    router_probs = shifted / jnp.sum(shifted, axis=-1, keepdims=True)
    return jnp.take_along_axis(router_probs, expert_ids, axis=1)


def split_heads(projected, images):
    shaped = projected.reshape(images, SEQ, 3, HEADS, HEAD_DIM)
    return (shaped[:, :, 0], shaped[:, :, 1], shaped[:, :, 2])


def attend_forward(projected, images):
    queries, keys_part, values_part = split_heads(projected, images)
    scores = (
        jnp.einsum("iqhd,ikhd->ihqk", queries, keys_part, preferred_element_type=jnp.float32)
        * 0.125
    )
    row_max = jnp.max(scores, axis=-1, keepdims=True)
    powered = jnp.exp(scores - row_max)
    row_total = jnp.sum(powered, axis=-1, keepdims=True)
    attn_probs = (powered / row_total).astype(jnp.bfloat16)
    mixed = jnp.einsum(
        "ihqk,ikhd->iqhd", attn_probs, values_part, preferred_element_type=jnp.float32
    )
    return (
        mixed.astype(jnp.bfloat16).reshape(images * SEQ, HEADS * HEAD_DIM),
        row_max + jnp.log(row_total),
    )


def attend_backward(projected, log_total, grad_mixed, images):
    queries, keys_part, values_part = split_heads(projected, images)
    grad_shaped = grad_mixed.reshape(images, SEQ, HEADS, HEAD_DIM)
    scores = (
        jnp.einsum("iqhd,ikhd->ihqk", queries, keys_part, preferred_element_type=jnp.float32)
        * 0.125
    )
    attn_probs = jnp.exp(scores - log_total)
    grad_probs = jnp.einsum(
        "iqhd,ikhd->ihqk", grad_shaped, values_part, preferred_element_type=jnp.float32
    )
    inner_sum = jnp.sum(attn_probs * grad_probs, axis=-1, keepdims=True)
    grad_scores = (attn_probs * (grad_probs - inner_sum)).astype(jnp.bfloat16)
    grad_queries = (
        jnp.einsum("ihqk,ikhd->iqhd", grad_scores, keys_part, preferred_element_type=jnp.float32)
        * 0.125
    )
    grad_keys = (
        jnp.einsum("ihqk,iqhd->ikhd", grad_scores, queries, preferred_element_type=jnp.float32)
        * 0.125
    )
    grad_values = jnp.einsum(
        "ihqk,iqhd->ikhd",
        attn_probs.astype(jnp.bfloat16),
        grad_shaped,
        preferred_element_type=jnp.float32,
    )
    stacked = jnp.stack([grad_queries, grad_keys, grad_values], axis=2)
    return stacked.reshape(images * SEQ, 3 * HEADS * HEAD_DIM).astype(jnp.bfloat16)


def per_device(
    block_input,
    attention_in,
    attention_out,
    expert_up,
    expert_down,
    router_weight,
    gain_attention,
    gain_experts,
    expert_ids,
    expert_slots,
    expert_capacity,
    keep_mask,
    output_grad,
):
    tok_rows = block_input.shape[0]
    model_width = block_input.shape[1]
    images = tok_rows // SEQ
    expert_count = expert_capacity.shape[0]
    capacity_rows = (2 * tok_rows * 11 // (8 * expert_count) + 7) // 8 * 8
    buffer_rows = expert_count * capacity_rows
    row_count = lax.axis_size("row")
    col_in, col_out = (
        lax.all_gather(attention_in, "col", axis=1, tiled=True),
        lax.all_gather(attention_out, "col", axis=1, tiled=True),
    )
    full_in, full_out = (
        lax.all_gather(col_in, "row", axis=0, tiled=True),
        lax.all_gather(col_out, "row", axis=0, tiled=True),
    )
    up_full, down_full = (
        lax.all_gather(expert_up, "col", axis=1, tiled=True),
        lax.all_gather(expert_down, "col", axis=2, tiled=True),
    )
    source = block_input.astype(jnp.float32)
    normed_one = norm_rows(source, gain_attention).astype(jnp.bfloat16)
    projected = jnp.dot(normed_one, full_in, preferred_element_type=jnp.float32).astype(
        jnp.bfloat16
    )
    mixed, log_total = attend_forward(projected, images)
    branch_attn = jnp.dot(mixed, full_out, preferred_element_type=jnp.float32)
    residual = source + branch_attn
    normed_two = norm_rows(residual, gain_experts)
    sent_rows = normed_two.astype(jnp.bfloat16)
    gate_values = route_gates(normed_two, router_weight, expert_ids)
    experts_iota = jnp.arange(expert_count, dtype=jnp.int32)
    limit_pairs = jnp.sum(
        jnp.where(
            expert_ids[:, :, None] == experts_iota[None, None, :], expert_capacity[None, None, :], 0
        ),
        axis=-1,
    )
    used_pairs = (keep_mask == 1) & (expert_slots < limit_pairs)
    slot_index = jnp.where(used_pairs, expert_ids * capacity_rows + expert_slots, buffer_rows)
    pair_table = (
        jnp.full((buffer_rows + 1,), 2 * tok_rows, jnp.int32)
        .at[slot_index.reshape(-1)]
        .set(jnp.arange(2 * tok_rows, dtype=jnp.int32))[:buffer_rows]
    )
    token_table = pair_table // 2
    padded_sent = jnp.concatenate([sent_rows, jnp.zeros((1, model_width), jnp.bfloat16)], axis=0)
    outgoing = padded_sent[token_table].reshape(expert_count, capacity_rows, model_width)
    arrived = lax.all_to_all(outgoing, "row", split_axis=0, concat_axis=0, tiled=True).reshape(
        row_count, EXP_DEV, capacity_rows, model_width
    )
    inner_act = jnp.einsum("rlcd,ldf->rlcf", arrived, up_full, preferred_element_type=jnp.float32)
    hidden = gelu_exact(inner_act).astype(jnp.bfloat16)
    returned = jnp.einsum(
        "rlcf,lfd->rlcd", hidden, down_full, preferred_element_type=jnp.float32
    ).astype(jnp.bfloat16)
    back_rows = lax.all_to_all(
        returned.reshape(expert_count, capacity_rows, model_width),
        "row",
        split_axis=0,
        concat_axis=0,
        tiled=True,
    )
    padded_back = jnp.concatenate(
        [back_rows.reshape(buffer_rows, model_width), jnp.zeros((1, model_width), jnp.bfloat16)],
        axis=0,
    )
    picked = padded_back[slot_index].astype(jnp.float32)
    weights_used = jnp.where(used_pairs, gate_values, 0.0)
    branch_moe = jnp.sum(weights_used[:, :, None] * picked, axis=1)
    result = residual + branch_moe
    grad_out = output_grad.astype(jnp.float32)
    grad_returned = (weights_used[:, :, None] * grad_out[:, None, :]).astype(jnp.bfloat16)
    grad_gates = jnp.where(used_pairs, jnp.sum(grad_out[:, None, :] * picked, axis=-1), 0.0)
    padded_grad = jnp.concatenate(
        [
            grad_returned.reshape(2 * tok_rows, model_width),
            jnp.zeros((1, model_width), jnp.bfloat16),
        ],
        axis=0,
    )
    grad_outgoing = padded_grad[pair_table].reshape(expert_count, capacity_rows, model_width)
    grad_arrived = lax.all_to_all(
        grad_outgoing, "row", split_axis=0, concat_axis=0, tiled=True
    ).reshape(row_count, EXP_DEV, capacity_rows, model_width)
    grad_hidden = jnp.einsum(
        "rlcd,lfd->rlcf", grad_arrived, down_full, preferred_element_type=jnp.float32
    )
    down_grad = jnp.einsum(
        "rlcf,rlcd->lfd", hidden, grad_arrived, preferred_element_type=jnp.float32
    )
    gelu_pull = jax.vjp(gelu_exact, inner_act)[1]
    grad_inner = gelu_pull(grad_hidden)[0].astype(jnp.bfloat16)
    up_grad = jnp.einsum("rlcd,rlcf->ldf", arrived, grad_inner, preferred_element_type=jnp.float32)
    grad_sent_rows = jnp.einsum(
        "rlcf,ldf->rlcd", grad_inner, up_full, preferred_element_type=jnp.float32
    ).astype(jnp.bfloat16)
    grad_back = lax.all_to_all(
        grad_sent_rows.reshape(expert_count, capacity_rows, model_width),
        "row",
        split_axis=0,
        concat_axis=0,
        tiled=True,
    )
    up_grad_local, down_grad_local = (
        lax.psum_scatter(
            up_grad.astype(jnp.bfloat16), "col", scatter_dimension=1, tiled=True
        ).astype(jnp.float32),
        lax.psum_scatter(
            down_grad.astype(jnp.bfloat16), "col", scatter_dimension=2, tiled=True
        ).astype(jnp.float32),
    )
    padded_token_grad = jnp.concatenate(
        [grad_back.reshape(buffer_rows, model_width), jnp.zeros((1, model_width), jnp.bfloat16)],
        axis=0,
    )
    grad_sent = jnp.sum(padded_token_grad[slot_index].astype(jnp.float32), axis=1)

    def route_part(normed, router_matrix):
        return route_gates(normed, router_matrix, expert_ids)

    route_pull = jax.vjp(route_part, normed_two, router_weight)[1]
    grad_normed_router, router_grad_part = route_pull(grad_gates)
    grad_normed_two = grad_sent + grad_normed_router
    norm_pull_two = jax.vjp(norm_rows, residual, gain_experts)[1]
    grad_residual_part, gain_experts_part = norm_pull_two(grad_normed_two)
    grad_residual = grad_out + grad_residual_part
    grad_branch = grad_residual.astype(jnp.bfloat16)
    out_grad_full = jnp.einsum("td,te->de", mixed, grad_branch, preferred_element_type=jnp.float32)
    grad_mixed = jnp.einsum(
        "te,de->td", grad_branch, full_out, preferred_element_type=jnp.float32
    ).astype(jnp.bfloat16)
    grad_projected = attend_backward(projected, log_total, grad_mixed, images)
    in_grad_full = jnp.einsum(
        "td,te->de", normed_one, grad_projected, preferred_element_type=jnp.float32
    )
    grad_normed_one = jnp.einsum(
        "te,de->td", grad_projected, full_in, preferred_element_type=jnp.float32
    )
    norm_pull_one = jax.vjp(norm_rows, source, gain_attention)[1]
    grad_source, gain_attention_part = norm_pull_one(grad_normed_one)
    input_grad = (grad_residual + grad_source).astype(jnp.bfloat16)
    in_partial, out_partial = (
        lax.psum_scatter(
            in_grad_full.astype(jnp.bfloat16), "row", scatter_dimension=0, tiled=True
        ).astype(jnp.float32),
        lax.psum_scatter(
            out_grad_full.astype(jnp.bfloat16), "row", scatter_dimension=0, tiled=True
        ).astype(jnp.float32),
    )
    in_grad_local, out_grad_local = (
        lax.psum_scatter(
            in_partial.astype(jnp.bfloat16), "col", scatter_dimension=1, tiled=True
        ).astype(jnp.float32),
        lax.psum_scatter(
            out_partial.astype(jnp.bfloat16), "col", scatter_dimension=1, tiled=True
        ).astype(jnp.float32),
    )
    square_parts = jnp.stack(
        [
            jnp.sum(result * result),
            jnp.sum(branch_attn * branch_attn),
            jnp.sum(branch_moe * branch_moe),
        ]
    )
    router_grad, gain_attention_grad, gain_experts_grad, square_sums = lax.psum(
        (router_grad_part, gain_attention_part, gain_experts_part, square_parts), ("row", "col")
    )
    token_total = tok_rows * lax.axis_size("row") * lax.axis_size("col")
    residual_rms = jnp.sqrt(square_sums / (token_total * model_width))
    return (
        result.astype(jnp.bfloat16),
        input_grad,
        in_grad_local,
        out_grad_local,
        up_grad_local,
        down_grad_local,
        router_grad,
        gain_attention_grad,
        gain_experts_grad,
        residual_rms,
    )


def solution(mesh):
    in_specs = (
        P(("row", "col"), None),
        P("row", "col"),
        P("row", "col"),
        P("row", "col", None),
        P("row", None, "col"),
        P(),
        P(),
        P(),
        P(("row", "col"), None),
        P(("row", "col"), None),
        P(),
        P(("row", "col"), None),
        P(("row", "col"), None),
    )
    out_specs = (
        P(("row", "col"), None),
        P(("row", "col"), None),
        P("row", "col"),
        P("row", "col"),
        P("row", "col", None),
        P("row", None, "col"),
        P(),
        P(),
        P(),
        P(),
    )
    return jax.shard_map(
        per_device, mesh=mesh, in_specs=in_specs, out_specs=out_specs, check_vma=False
    )
```

profile of v0, /device:TPU:0, one launch (start us, length us, event | category | flops | bytes accessed | tf_op | source)
XLA Modules:
  0.0 836.2 jit_solution(14805286641179050180)
XLA Ops:
  25.6 38.8 %all-gather.5.cloned.1.call-done = bf16[768,2304]{1,0:T(8,128)(2,1)} async-done(((bf16[48,2304]{1,0:T(8,128)(2,1)}), bf16[768,2304]{1,0:T(8,128)(2,1)}) %all-gather.5.cloned.1.call-update) | async-done | bytes 3538960 | tf_op jit(solution)/shard_map/all_gather | solution.py:115
  71.2 11.9 %reshape.324 = bf16[4,197,3,12,64]{4,3,2,1,0:T(8,128)(2,1)} reshape(bf16[788,2304]{1,0:T(8,128)(2,1)} %convolution_convert_fusion) | data formatting | bytes 7262208 | tf_op jit(solution)/shard_map/reshape | solution.py:34
  132.4 20.0 %gather_fusion.4 = f32[1576]{0:T(1024)S(1)} fusion(f32[788,16]{0,1:T(8,128)S(1)} %get-tuple-element.41, s32[1576]{0:T(1024)S(1)} %reshape.284), kind=kCustom, calls=%fused_computation.4 | custom fusion | bytes 25216 | tf_op jit(solution)/shard_map/jit(take_along_axis)/gather | solution.py:30
  198.7 38.8 %all-to-all-done = bf16[16,136,768]{2,1,0:T(8,128)(2,1)} async-done(((bf16[16,136,768]{2,1,0:T(8,128)(2,1)}), bf16[16,136,768]{2,1,0:T(8,128)(2,1)}, u32[]{:S(2)}, u32[]{:S(2)}) %all-to-all-start) | async-done | bytes 3342368 | tf_op jit(solution)/shard_map/all_to_all | solution.py:150
  237.5 16.4 %all-to-all-start.2 = ((bf16[16,136,768]{2,1,0:T(8,128)(2,1)}), bf16[16,136,768]{2,1,0:T(8,128)(2,1)S(1)}, u32[]{:S(2)}, u32[]{:S(2)}) async-start(bf16[16,136,768]{2,1,0:T(8,128)(2,1)} %bitcast.130), calls=%async_computation.2 | async-start | bytes 6684672 | tf_op jit(solution)/shard_map/all_to_all | solution.py:184
  254.0 21.0 %multiply_convert_fusion = (bf16[16,136,3072]{2,1,0:T(8,128)(2,1)}, f32[16,136,3072]{2,1,0:T(8,128)}) fusion(bf16[16,136,768]{2,1,0:T(8,128)(2,1)} %all-to-all-done, bf16[1,768,3072]{2,1,0:T(8,128)(2,1)} %all-gather.9.cloned.1.call-done), kind=kOutput, calls=%fused_computation.8 | convolution fusion | flops 10301079552 | bytes 48168960 | tf_op jit(solution)/shard_map/rlcd,ldf->rlcf/dot_general | solution.py:153
  275.0 29.4 %all-gather.11.cloned.1.call-done = bf16[1,3072,768]{2,1,0:T(8,128)(2,1)} async-done(((bf16[1,3072,384]{2,1,0:T(8,128)(2,1)}), bf16[1,3072,768]{2,1,0:T(8,128)(2,1)}) %all-gather.11.cloned.1.call-update) | async-done | bytes 4718608 | tf_op jit(solution)/shard_map/all_gather | solution.py:120
  304.4 16.2 %fusion.29 = bf16[16,136,768]{2,1,0:T(8,128)(2,1)} fusion(bf16[16,136,3072]{2,1,0:T(8,128)(2,1)} %get-tuple-element.49, bf16[1,3072,768]{2,1,0:T(8,128)(2,1)} %all-gather.11.cloned.1.call-done), kind=kOutput, calls=%fused_computation.67 | convolution fusion | flops 10269327360 | bytes 21430272 | tf_op jit(solution)/shard_map/rlcf,lfd->rlcd/dot_general | solution.py:155
  322.4 12.6 %all-to-all-start.1 = ((bf16[16,136,768]{2,1,0:T(8,128)(2,1)}), bf16[16,136,768]{2,1,0:T(8,128)(2,1)S(1)}, u32[]{:S(2)}, u32[]{:S(2)}) async-start(bf16[16,136,768]{2,1,0:T(8,128)(2,1)} %fusion.29), calls=%async_computation.1 | async-start | bytes 6684672 | tf_op jit(solution)/shard_map/all_to_all | solution.py:158
  334.9 26.1 %add_convert_fusion = bf16[16,136,3072]{2,1,0:T(8,128)(2,1)S(1)} fusion(f32[16,136,3072]{2,1,0:T(8,128)} %get-tuple-element.50, bf16[16,136,768]{2,1,0:T(8,128)(2,1)} %copy-done.21, bf16[1,3072,768]{2,1,0:T(8,128)(2,1)} %all-gather.11.cloned.1.call-done), kind=kOutput, calls=%fused_computation.7 | convolution fusion | flops 10354556928 | bytes 48168960 | tf_op jit(solution)/shard_map/rlcd,lfd->rlcf/dot_general | solution.py:187
  365.8 16.1 %fusion.26 = bf16[16,136,768]{2,1,0:T(8,128)(2,1)} fusion(bf16[16,136,3072]{2,1,0:T(8,128)(2,1)S(1)} %add_convert_fusion, bf16[1,768,3072]{2,1,0:T(8,128)(2,1)} %all-gather.9.cloned.1.call-done), kind=kOutput, calls=%fused_computation.66 | convolution fusion | flops 10269327360 | bytes 21430272 | tf_op jit(solution)/shard_map/rlcf,ldf->rlcd/dot_general | solution.py:196
  381.9 15.8 %all-to-all-done.1 = bf16[16,136,768]{2,1,0:T(8,128)(2,1)S(1)} async-done(((bf16[16,136,768]{2,1,0:T(8,128)(2,1)}), bf16[16,136,768]{2,1,0:T(8,128)(2,1)S(1)}, u32[]{:S(2)}, u32[]{:S(2)}) %all-to-all-start.1) | async-done | bytes 3342368 | tf_op jit(solution)/shard_map/all_to_all | solution.py:158
  399.4 16.3 %all-to-all-start.3 = ((bf16[16,136,768]{2,1,0:T(8,128)(2,1)}), bf16[16,136,768]{2,1,0:T(8,128)(2,1)}, u32[]{:S(2)}, u32[]{:S(2)}) async-start(bf16[16,136,768]{2,1,0:T(8,128)(2,1)} %fusion.26), calls=%async_computation.3 | async-start | bytes 6684672 | tf_op jit(solution)/shard_map/all_to_all | solution.py:199
  435.3 13.7 %multiply_reduce_fusion.2 = (f32[788,2]{1,0:T(8,128)S(1)}, f32[788,768]{1,0:T(8,128)}) fusion(f32[788,2,768]{2,1,0:T(2,128)} %reshape.311, f32[788,768]{1,0:T(8,128)S(1)} %copy-done.15, f32[788,2]{1,0:T(8,128)S(1)} %copy-done.20), kind=kLoop, calls=%fused_computation.26 | loop fusion | flops 4234712 | bytes 9695552 | tf_op jit(solution)/shard_map/reduce_sum | solution.py:175
  459.8 18.7 %all-to-all-done.3 = bf16[16,136,768]{2,1,0:T(8,128)(2,1)} async-done(((bf16[16,136,768]{2,1,0:T(8,128)(2,1)}), bf16[16,136,768]{2,1,0:T(8,128)(2,1)}, u32[]{:S(2)}, u32[]{:S(2)}) %all-to-all-start.3) | async-done | bytes 3342368 | tf_op jit(solution)/shard_map/all_to_all | solution.py:199
  541.5 12.1 %multiply_convert_fusion.1 = bf16[4,12,197,197]{2,3,1,0:T(8,128)(2,1)} fusion(f32[4,12,197,197]{2,3,1,0:T(8,128)} %get-tuple-element.53, f32[4,12,197,197]{2,3,1,0:T(8,128)} %get-tuple-element.46, f32[4,12,197]{2,1,0:T(8,128)S(1)} %get-tuple-element.52, f32[4,12,197]{2,1,0:T(8,128)S(1)} %log_add_fusion), kind=kLoop, calls=%fused_computation.10 | loop fusion | flops 9314160 | bytes 18703968 | tf_op jit(solution)/shard_map/convert_element_type | solution.py:69
  583.9 16.3 %reduce-scatter.15.cloned.1.call-done = bf16[48,768]{1,0:T(8,128)(2,1)} async-done(((bf16[768,768]{1,0:T(8,128)(2,1)}), bf16[48,768]{1,0:T(8,128)(2,1)}) %reduce-scatter.15.cloned.1.call-update) | async-done | bytes 73744 | tf_op jit(solution)/shard_map/reduce_scatter | solution.py:248
  610.7 17.0 %fusion.15 = bf16[1,3072,768]{2,1,0:T(8,128)(2,1)} fusion(bf16[16,136,3072]{2,1,0:T(8,128)(2,1)} %get-tuple-element.49, bf16[16,136,768]{2,1,0:T(8,128)(2,1)} %copy-done.21), kind=kOutput, calls=%fused_computation.40 | convolution fusion | flops 10270015488 | bytes 21430272 | tf_op jit(solution)/shard_map/rlcf,rlcd->lfd/dot_general | solution.py:190
  627.7 20.5 %copy.172 = bf16[1,3072,768]{1,0,2:T(2,128)(2,1)} copy(bf16[1,3072,768]{2,1,0:T(8,128)(2,1)} %fusion.15) | data formatting | bytes 9437184
  655.9 17.1 %fusion.14 = bf16[1,768,3072]{2,1,0:T(8,128)(2,1)} fusion(bf16[16,136,768]{2,1,0:T(8,128)(2,1)} %all-to-all-done, bf16[16,136,3072]{2,1,0:T(8,128)(2,1)} %copy-done.61), kind=kOutput, calls=%fused_computation.39 | convolution fusion | flops 10270015488 | bytes 21430272 | tf_op jit(solution)/shard_map/rlcd,rlcf->ldf/dot_general | solution.py:195
  685.8 41.9 %all-reduce.4 = (f32[768,16]{0,1:T(8,128)}, f32[768]{0:T(1024)}, f32[768]{0:T(1024)}, f32[3]{0:T(128)S(1)}) all-reduce(f32[768,16]{0,1:T(8,128)S(1)} %fusion.32, f32[768]{0:T(1024)S(1)} %get-tuple-element.14, f32[768]{0:T(1024)S(1)} %get-tuple-element.19, f32[3]{0:T(128)S(1)} %pad_maximum_fusion.1), channel_id=1, replica_groups=mesh['row'=16,'col'=2] {'row','col'}, use_global_device_ids=true, to_apply=%region_28.29 | all-reduce | flops 13827 | bytes 110616 | tf_op jit(solution)/shard_map/psum | solution.py:267
  735.7 11.1 %reduce-scatter.23.cloned.1.call-done = bf16[384,3072]{1,0:T(8,128)(2,1)} async-done(((bf16[768,3072]{1,0:T(8,128)(2,1)}), bf16[384,3072]{1,0:T(8,128)(2,1)}) %reduce-scatter.23.cloned.1.call-update) | async-done | bytes 2359312
  765.0 44.7 %reduce-scatter.17.cloned.1.call-done = bf16[1,384,3072]{2,1,0:T(8,128)(2,1)} async-done(((bf16[1,768,3072]{2,1,0:T(8,128)(2,1)}), bf16[1,384,3072]{2,1,0:T(8,128)(2,1)}) %reduce-scatter.17.cloned.1.call-update) | async-done | bytes 2359312 | tf_op jit(solution)/shard_map/reduce_scatter | solution.py:207
  814.1 12.9 %reduce-scatter.19.cloned.1.call-done = bf16[1152,48]{1,0:T(8,128)(2,1)} async-done(((bf16[2304,48]{1,0:T(8,128)(2,1)}), bf16[1152,48]{1,0:T(8,128)(2,1)}) %reduce-scatter.19.cloned.1.call-update) | async-done | bytes 110608
  (264 shorter events, 314.2 us)
Async XLA Ops:
  8.0 120.5 %copy-start = (f32[768,16]{0,1:T(8,128)S(1)}, f32[768,16]{0,1:T(8,128)}, u32[]{:S(2)}) copy-start(f32[768,16]{0,1:T(8,128)} %param.18) | copy-start | bytes 147460
  8.1 56.4 %copy-start.55 = (f32[768]{0:T(1024)S(1)}, f32[768]{0:T(1024)}, u32[]{:S(2)}) copy-start(f32[768]{0:T(1024)} %param.19) | copy-start | bytes 9220
  8.1 56.4 %all-gather.5.cloned.1.call-start = ((), (), s32[]{:S(2)}) async-start(), calls=%async_computation.10 | async-start | bytes 3760128 | tf_op jit(solution)/shard_map/all_gather | solution.py:115
  16.8 106.2 %all-gather.7.cloned.1.call-start = ((), (), s32[]{:S(2)}) async-start(), calls=%async_computation.11 | async-start | bytes 1253376 | tf_op jit(solution)/shard_map/all_gather | solution.py:116
  23.4 47.9 %copy-start.42 = (f32[788]{0:T(1024)}, f32[788]{0:T(1024)S(1)}, u32[]{:S(2)}) copy-start(f32[788]{0:T(1024)S(1)} %broadcast_multiply_fusion.1) | copy-start | bytes 9460
  24.5 46.7 %copy-start.48 = (f32[788]{0:T(1024)}, f32[788]{0:T(1024)S(1)}, u32[]{:S(2)}) copy-start(f32[788]{0:T(1024)S(1)} %fusion.84) | copy-start | bytes 9460
  170.2 67.3 %all-to-all-start = ((bf16[16,136,768]{2,1,0:T(8,128)(2,1)}), bf16[16,136,768]{2,1,0:T(8,128)(2,1)}, u32[]{:S(2)}, u32[]{:S(2)}) async-start(bf16[16,136,768]{2,1,0:T(8,128)(2,1)} %bitcast.129), calls=%async_computation | async-start | bytes 6684672 | tf_op jit(solution)/shard_map/all_to_all | solution.py:150
  174.7 79.2 %all-gather.9.cloned.1.call-start = ((), (), s32[]{:S(2)}) async-start(), calls=%async_computation.12 | async-start | bytes 7077888 | tf_op jit(solution)/shard_map/all_gather | solution.py:119
  175.3 129.1 %all-gather.11.cloned.1.call-start = ((), (), s32[]{:S(2)}) async-start(), calls=%async_computation.13 | async-start | bytes 7077888 | tf_op jit(solution)/shard_map/all_gather | solution.py:120
  237.5 83.1 %all-to-all-start.2 = ((bf16[16,136,768]{2,1,0:T(8,128)(2,1)}), bf16[16,136,768]{2,1,0:T(8,128)(2,1)S(1)}, u32[]{:S(2)}, u32[]{:S(2)}) async-start(bf16[16,136,768]{2,1,0:T(8,128)(2,1)} %bitcast.130), calls=%async_computation.2 | async-start | bytes 6684672 | tf_op jit(solution)/shard_map/all_to_all | solution.py:184
  322.4 75.3 %all-to-all-start.1 = ((bf16[16,136,768]{2,1,0:T(8,128)(2,1)}), bf16[16,136,768]{2,1,0:T(8,128)(2,1)S(1)}, u32[]{:S(2)}, u32[]{:S(2)}) async-start(bf16[16,136,768]{2,1,0:T(8,128)(2,1)} %fusion.29), calls=%async_computation.1 | async-start | bytes 6684672 | tf_op jit(solution)/shard_map/all_to_all | solution.py:158
  399.4 79.1 %all-to-all-start.3 = ((bf16[16,136,768]{2,1,0:T(8,128)(2,1)}), bf16[16,136,768]{2,1,0:T(8,128)(2,1)}, u32[]{:S(2)}, u32[]{:S(2)}) async-start(bf16[16,136,768]{2,1,0:T(8,128)(2,1)} %fusion.26), calls=%async_computation.3 | async-start | bytes 6684672 | tf_op jit(solution)/shard_map/all_to_all | solution.py:199
  415.8 184.4 %reduce-scatter.15.cloned.1.call-start = ((), (), s32[]{:S(2)}) async-start(), calls=%async_computation.15 | async-start | bytes 1253376 | tf_op jit(solution)/shard_map/reduce_scatter | solution.py:248
  435.3 24.4 %copy-start.23 = (f32[788,16]{0,1:T(8,128)S(1)}, f32[788,16]{0,1:T(8,128)}, u32[]{:S(2)}) copy-start(f32[788,16]{0,1:T(8,128)} %copy-done.22) | copy-start | bytes 151300
  530.4 201.7 %reduce-scatter.21.cloned.1.call-start = ((), (), s32[]{:S(2)}) async-start(), calls=%async_computation.18 | async-start | bytes 294912
  574.3 27.7 %copy-start.43 = (f32[788]{0:T(1024)S(1)}, f32[788]{0:T(1024)}, u32[]{:S(2)}) copy-start(f32[788]{0:T(1024)} %copy-done.42) | copy-start | bytes 9460
  574.3 27.7 %copy-start.49 = (f32[788]{0:T(1024)S(1)}, f32[788]{0:T(1024)}, u32[]{:S(2)}) copy-start(f32[788]{0:T(1024)} %copy-done.48) | copy-start | bytes 9460
  574.3 27.7 %copy-start.56 = (f32[768]{0:T(1024)S(1)}, f32[768]{0:T(1024)}, u32[]{:S(2)}) copy-start(f32[768]{0:T(1024)} %param.19) | copy-start | bytes 9220
  601.9 131.8 %reduce-scatter.13.cloned.1.call-start = ((), (), s32[]{:S(2)}) async-start(), calls=%async_computation.14 | async-start | bytes 3760128 | tf_op jit(solution)/shard_map/reduce_scatter | solution.py:245
  610.7 136.2 %reduce-scatter.23.cloned.1.call-start = ((), (), s32[]{:S(2)}) async-start(), calls=%async_computation.19 | async-start | bytes 7077888
  655.9 153.8 %reduce-scatter.17.cloned.1.call-start = ((), (), s32[]{:S(2)}) async-start(), calls=%async_computation.16 | async-start | bytes 7077888 | tf_op jit(solution)/shard_map/reduce_scatter | solution.py:207
  673.1 153.9 %reduce-scatter.19.cloned.1.call-start = ((), (), s32[]{:S(2)}) async-start(), calls=%async_computation.17 | async-start | bytes 884736
  684.3 44.0 %copy-start.7 = (bf16[788,768]{1,0:T(8,128)(2,1)S(1)}, bf16[788,768]{1,0:T(8,128)(2,1)}, u32[]{:S(2)}) copy-start(bf16[788,768]{1,0:T(8,128)(2,1)} %param.13) | copy-start | bytes 3631108
  684.3 43.9 %copy-start.14 = (bf16[788,768]{1,0:T(8,128)(2,1)S(1)}, bf16[788,768]{1,0:T(8,128)(2,1)}, u32[]{:S(2)}) copy-start(bf16[788,768]{1,0:T(8,128)(2,1)} %param.25) | copy-start | bytes 3631108
  (52 other events, 369.3 us)
Sparse Core Ops, SparseCore 0:
  16.9 47.5 all-gather.4
  66.7 37.3 all-gather.6
  530.5 69.6 reduce-scatter.14
Sparse Core Ops, SparseCore 1:
  176.8 63.6 all-gather.8
  241.9 62.5 all-gather.10
  602.0 9.8 reduce-scatter.20
  615.8 67.8 reduce-scatter.12
  686.5 60.2 reduce-scatter.22
  749.8 59.8 reduce-scatter.16
  811.8 15.2 reduce-scatter.18
where the time goes:
time: 848 us; the launch traced here: 836 us
  waiting for transfers between devices  228 us (27%)
  local copies, waits for them, and re-layouts  214 us (25%)
  matrix products  191 us (23%)
  other arithmetic  81.6 us (10%)
  blocking collectives  55.4 us (7%)
  starting transfers between devices  50.2 us (6%)
  between operations  16.6 us (2%)
    unnamed x137, local copies, waits for them, and re-layouts  77 us
    reduce_scatter x1, waiting for transfers between devices, per_device(): lax.psum_scatter(up_grad.astype(jnp.bfloat16), 'col', scatter_dimension=1...  44.7 us
    psum x1, blocking collectives, per_device(): lax.psum((router_grad_part, gain_attention_part, gain_experts_part, squar...  41.9 us
    all_gather x1, waiting for transfers between devices, per_device(): lax.all_gather(col_in, 'row', axis=0, tiled=True)  38.8 us
    all_to_all x1, waiting for transfers between devices, per_device(): lax.all_to_all(outgoing, 'row', split_axis=0, concat_axis=0, tiled=True)  38.8 us
    all_gather x1, waiting for transfers between devices, per_device(): lax.all_gather(expert_down, 'col', axis=2, tiled=True)  29.4 us
    dot_general x1, matrix products, per_device(): jnp.einsum('rlcd,lfd->rlcf', grad_arrived, down_full, preferred_element_t...  26.1 us
    unnamed x13, waiting for transfers between devices  25.2 us
  transfers between devices with their start and end apart: 14, of which 9 were waited for; matrix products, arithmetic and copies ran while one was open for 45% of the time, Pallas kernels for 0%

commit v1 on v0

v1 whole, which is shorter than its diff:
```python
import functools

import jax
import jax.numpy as jnp
from jax import lax
from jax.experimental import pallas as pl
from jax.experimental.pallas import tpu as pltpu
from jax.sharding import PartitionSpec as P

HEADS = 12
HEAD_DIM = 64
SEQ = 197
EPS = 1e-06
F32 = jnp.float32
BF16 = jnp.bfloat16
WIN = 224
STEP = 192
NEG = -1e30
MIB = 1 << 20

VMEM = pl.BlockSpec(memory_space=pltpu.VMEM)
ANY = pl.BlockSpec(memory_space=pl.ANY)
MESH = pl.DeviceIdType.MESH
DMA = pltpu.SemaphoreType.DMA


def dot(a, b):
    return jnp.dot(a, b, preferred_element_type=F32)


def dot_nt(a, b):
    return lax.dot_general(a, b, (((1,), (1,)), ((), ())), preferred_element_type=F32)


def dot_tn(a, b):
    return lax.dot_general(a, b, (((0,), (0,)), ((), ())), preferred_element_type=F32)


def cdiv(a, b):
    return (a + b - 1) // b


def params(mib, **kw):
    return pltpu.CompilerParams(vmem_limit_bytes=mib * MIB, **kw)


def split_bf16(v):
    hi = v.astype(BF16)
    return hi, (v - hi.astype(F32)).astype(BF16)


def load_blocks(g_hbm, dst, sem):
    blocks, rh, cw = g_hbm.shape
    nc = dst.shape[1] // cw
    for b in range(blocks):
        r, c = divmod(b, nc)
        pltpu.make_async_copy(
            g_hbm.at[b], dst.at[pl.ds(r * rh, rh), pl.ds(c * cw, cw)], sem
        ).start()


def wait_all(dst, sem):
    pltpu.make_async_copy(dst, dst, sem).wait()


def row_loop(total, step, body):
    @pl.loop(0, total // step)
    def _(i):
        body(pl.ds(pl.multiple_of(i * step, step), step))


def pad_rows(src_ref, dst_ref):
    rows, padded = src_ref.shape[0], dst_ref.shape[0]
    tail = rows // 16 * 16
    dst_ref[tail:padded, :] = jnp.zeros((padded - tail, dst_ref.shape[1]), dst_ref.dtype)
    dst_ref[0:rows, :] = src_ref[...]


def norm_parts(v):
    c = v - jnp.mean(v, axis=-1, keepdims=True)
    r = lax.rsqrt(jnp.mean(c * c, axis=-1, keepdims=True) + EPS)
    return c * r, r


def slot_hits(slot_ref, base, rows):
    lanes = slot_ref.shape[1]
    at = lax.broadcasted_iota(jnp.int32, (rows, lanes), 0) + base
    return at == slot_ref[0:1, :], at == slot_ref[1:2, :]


def mesh_place():
    r, c = lax.axis_index("row"), lax.axis_index("col")
    return r // 4, (r // 2) % 2, r % 2, c


def device(z, y, k, c):
    return {"row": z * 4 + y * 2 + k, "col": c}


def greet(peers):
    barrier = pltpu.get_barrier_semaphore()
    for peer in peers:
        pl.semaphore_signal(barrier, inc=1, device_id=peer, device_id_type=MESH)
    pl.semaphore_wait(barrier, len(peers))


def push(src, dst, send, recv, peer):
    copy = pltpu.make_async_remote_copy(
        src_ref=src, dst_ref=dst, send_sem=send, recv_sem=recv, device_id=peer, device_id_type=MESH
    )
    copy.start()
    return copy


def zflip(z, d):
    bit0, bit1 = z % 2, z // 2
    if d & 1:
        bit0 = 1 - bit0
    if d & 2:
        bit1 = 1 - bit1
    return bit1 * 2 + bit0


def peers_of(z, y, k, c):
    return [device(zflip(z, d), y, k, c) for d in (1, 2, 3)] + [
        device(z, y, 1 - k, c), device(z, y, k, 1 - c), device(z, 1 - y, k, c)
    ]


def gather_kernel(own_ref, g_ref, zs, zr, xs, xr, ys, yr, ks, kr, own_sem):
    z, y, k, c = mesh_place()
    rh, half = own_ref.shape[0], own_ref.shape[1] // 2
    greet(peers_of(z, y, k, c))
    across, up, twin = device(z, y, k, 1 - c), device(z, 1 - y, k, c), device(z, y, 1 - k, c)

    def at(zz, yy, kk, cc, cols=None):
        rows = pl.ds(pl.multiple_of((zz * 4 + yy * 2 + kk) * rh, rh), rh)
        if cols is None:
            return g_ref.at[cc, rows, :]
        return g_ref.at[cc, rows, cols]

    h1, h2 = pl.ds(0, half), pl.ds(half, half)
    mine = at(z, y, k, c)
    zc = [push(own_ref, mine, zs.at[d - 1], zr.at[d - 1], device(zflip(z, d), y, k, c)) for d in (1, 2, 3)]
    keep = pltpu.make_async_copy(own_ref, mine, own_sem)
    keep.start()
    sent = list(zc)
    xc, yc, kc, xf, yf = [], [], [], [], []
    for d in range(4):
        zz = zflip(z, d)
        if d:
            zc[d - 1].wait_recv()
        src = own_ref if d == 0 else at(zz, y, k, c)
        xc.append(push(src, at(zz, y, k, c), xs.at[d], xr.at[d], across))
        yc.append(push(src, at(zz, y, k, c), ys.at[d], yr.at[d], up))
        kc.append(push(src, at(zz, y, k, c), ks.at[d], kr.at[d], twin))
    for d in range(4):
        zz = zflip(z, d)
        xc[d].wait_recv()
        src = at(zz, y, k, 1 - c)
        yf.append(push(at(zz, y, k, 1 - c, h1), at(zz, y, k, 1 - c, h1), ys.at[4 + d], yr.at[4 + d], up))
        kc.append(push(src, src, ks.at[4 + d], kr.at[4 + d], twin))
        yc[d].wait_recv()
        src = at(zz, 1 - y, k, c)
        xf.append(push(at(zz, 1 - y, k, c, h2), at(zz, 1 - y, k, c, h2), xs.at[4 + d], xr.at[4 + d], across))
        kc.append(push(src, src, ks.at[8 + d], kr.at[8 + d], twin))
    for d in range(4):
        yf[d].wait_recv()
        xf[d].wait_recv()
        src = at(zflip(z, d), 1 - y, k, 1 - c)
        kc.append(push(src, src, ks.at[12 + d], kr.at[12 + d], twin))
    for copy in kc:
        copy.wait_recv()
    for copy in zc + xc + yc + xf + yf + kc:
        copy.wait_send()
    keep.wait()


def reduce_kernel(
    w_ref, small_ref, out_ref, small_out,
    rk, acc, rx2, ry2, rx3, ry3, rz, cur, rs,
    ks, kr, xs, xr, ys, yr, zs, zr, ss, sr,
):
    z, y, k, c = mesh_place()
    rh, half = out_ref.shape[0], out_ref.shape[1] // 2
    greet(peers_of(z, y, k, c))
    across, up, twin = device(z, y, k, 1 - c), device(z, 1 - y, k, c), device(z, y, 1 - k, c)
    order = (3, 2, 1, 0)
    lo, hi = pl.ds(0, half), pl.ds(half, half)

    def rows(zz, yy, kk):
        return pl.ds(pl.multiple_of((zz * 4 + yy * 2 + kk) * rh, rh), rh)

    chain = [twin, across, up, device(zflip(z, 1), y, k, c), device(zflip(z, 2), y, k, c)]
    small = []
    cur[0] = small_ref[...]

    def small_send():
        j = len(small)
        small.append(push(cur.at[j], rs.at[j], ss.at[j], sr.at[j], chain[j]))

    def small_take():
        j = len(small) - 1
        small[j].wait_recv()
        cur[j + 1] = cur[j] + rs[j]

    kc = {}
    for d in order:
        zz = zflip(z, d)
        for yy in range(2):
            for cc in range(2):
                n = yy * 2 + cc
                kc[d, yy, cc] = push(
                    w_ref.at[cc, rows(zz, yy, 1 - k), :], rk.at[d, yy, cc], ks.at[d * 4 + n], kr.at[d * 4 + n], twin
                )
    small_send()
    c2x, c2y, c3x, c3y, cz = {}, {}, {}, {}, {}
    for d in order:
        zz = zflip(z, d)
        for yy in range(2):
            for cc in range(2):
                kc[d, yy, cc].wait_recv()
                acc[d, yy, cc] = (
                    w_ref[cc, rows(zz, yy, k), :].astype(F32) + rk[d, yy, cc].astype(F32)
                ).astype(BF16)
        c2y[d] = push(acc.at[d, 1 - y, :, :, lo], ry2.at[d], ys.at[d], yr.at[d], up)
        c2x[d] = push(acc.at[d, :, 1 - c, :, hi], rx2.at[d], xs.at[d], xr.at[d], across)
    small_take()
    small_send()
    for d in order:
        c2y[d].wait_recv()
        for cc in range(2):
            acc[d, y, cc, :, 0:half] = (
                acc[d, y, cc, :, 0:half].astype(F32) + ry2[d, cc].astype(F32)
            ).astype(BF16)
        c3x[d] = push(acc.at[d, y, 1 - c, :, lo], rx3.at[d], xs.at[4 + d], xr.at[4 + d], across)
        c2x[d].wait_recv()
        for yy in range(2):
            acc[d, yy, c, :, half:] = (
                acc[d, yy, c, :, half:].astype(F32) + rx2[d, yy].astype(F32)
            ).astype(BF16)
        c3y[d] = push(acc.at[d, 1 - y, c, :, hi], ry3.at[d], ys.at[4 + d], yr.at[4 + d], up)
    small_take()
    small_send()
    for d in order:
        c3x[d].wait_recv()
        acc[d, y, c, :, 0:half] = (
            acc[d, y, c, :, 0:half].astype(F32) + rx3[d].astype(F32)
        ).astype(BF16)
        c3y[d].wait_recv()
        acc[d, y, c, :, half:] = (
            acc[d, y, c, :, half:].astype(F32) + ry3[d].astype(F32)
        ).astype(BF16)
        if d:
            cz[d] = push(acc.at[d, y, c], rz.at[d - 1], zs.at[d - 1], zr.at[d - 1], device(zflip(z, d), y, k, c))
    small_take()
    small_send()
    small_take()
    small_send()
    total = acc[0, y, c].astype(F32)
    for d in (1, 2, 3):
        cz[d].wait_recv()
        total += rz[d - 1].astype(F32)
    out_ref[...] = total
    small[4].wait_recv()
    small_out[...] = cur[4] + rs[4]
    for group in (kc, c2x, c2y, c3x, c3y, cz):
        for copy in group.values():
            copy.wait_send()
    for copy in small:
        copy.wait_send()


def dispatch_kernel(blocks, src_ref, slot_ref, out_ref, pad):
    pad_rows(src_ref, pad)
    rows = out_ref.shape[0] // blocks

    @pl.loop(0, blocks)
    def _(b):
        base = pl.multiple_of(b * rows, 16)
        h0, h1 = slot_hits(slot_ref, base, rows)
        pick = jnp.where(h0 | h1, 1.0, 0.0).astype(BF16)
        out_ref[pl.ds(base, rows), :] = dot(pick, pad[...]).astype(BF16)


def forward_kernel(
    images, experts, blocks,
    x_ref, wt_ref, g1_ref, g2_ref, rw_ref, slot_ref,
    proj_ref, mixed_ref, lse_ref, res_ref, probs_ref, tok_ref, sq_ref,
    n1, xs, sent, low,
):
    padded, width = xs.shape
    nc = wt_ref.shape[0]
    cw, ow = 3 * width // nc, width // nc
    pad_rows(x_ref, xs)

    def norm_one(rows):
        n, _ = norm_parts(xs[rows, :].astype(F32))
        n1[rows, :] = (n * g1_ref[...]).astype(BF16)

    row_loop(padded, 32, norm_one)
    mixed_ref[...] = jnp.zeros_like(mixed_ref)
    lse_ref[...] = jnp.zeros_like(lse_ref)
    for c in range(nc):
        proj_ref[:, c * cw : (c + 1) * cw] = dot(n1[...], wt_ref[c, :, 0:cw]).astype(BF16)

    lane = lax.broadcasted_iota(jnp.int32, (1, 128), 1)
    first = lane < HEAD_DIM
    key_at = lax.broadcasted_iota(jnp.int32, (1, WIN), 1)
    row_at = lax.broadcasted_iota(jnp.int32, (WIN, 1), 0)

    @pl.loop(0, HEADS // 2)
    def _(p):
        qc = pl.ds(pl.multiple_of(p * 128, 128), 128)
        kc = pl.ds(pl.multiple_of(width + p * 128, 128), 128)
        vc = pl.ds(pl.multiple_of(2 * width + p * 128, 128), 128)
        for i in range(images):
            rows = slice(STEP * i, STEP * i + WIN)
            off = (SEQ - STEP) * i
            bias = jnp.where((key_at >= off) & (key_at < off + SEQ), 0.0, NEG)
            valid = (row_at >= off) & (row_at < off + SEQ)
            q = (proj_ref[rows, qc].astype(F32) * 0.125)
            qq = jnp.concatenate([jnp.where(first, q, 0.0), jnp.where(first, 0.0, q)], axis=0).astype(BF16)
            s = dot_nt(qq, proj_ref[rows, kc]) + bias
            top = jnp.max(s, axis=1, keepdims=True)
            e = jnp.exp(s - top)
            total = jnp.sum(e, axis=1, keepdims=True)
            o = dot(e.astype(BF16), proj_ref[rows, vc]) / total
            lse = top + jnp.log(total)
            om = jnp.where(first, o[:WIN], o[WIN:])
            old = mixed_ref[rows, qc].astype(F32)
            mixed_ref[rows, qc] = jnp.where(valid, om, old).astype(BF16)
            ls = lse_ref[rows, :]
            ls = jnp.where(valid & (lane == 2 * p), lse[:WIN], ls)
            lse_ref[rows, :] = jnp.where(valid & (lane == 2 * p + 1), lse[WIN:], ls)

    for c in range(nc):
        cols = slice(c * ow, (c + 1) * ow)
        branch = dot(mixed_ref[...], wt_ref[c, :, cw:])
        sq_ref[:, cols] = jnp.sum(branch * branch, axis=0, keepdims=True)
        res_ref[:, cols] = xs[:, cols].astype(F32) + branch

    def norm_two(rows):
        n, _ = norm_parts(res_ref[rows, :])
        v = n * g2_ref[...]
        hi, lo = split_bf16(v)
        sent[rows, :] = hi
        low[rows, :] = lo

    row_loop(padded, 32, norm_two)
    rw_hi, rw_lo = split_bf16(rw_ref[...])
    both = dot_nt(jnp.concatenate([rw_hi, rw_lo], axis=0), sent[...])
    logits = both[:experts] + both[experts:] + dot_nt(rw_hi, low[...])
    e = jnp.exp(logits - jnp.max(logits, axis=0, keepdims=True))
    probs = e / jnp.sum(e, axis=0, keepdims=True)
    probs_ref[...] = probs
    rows = tok_ref.shape[0] // blocks

    @pl.loop(0, blocks)
    def _(b):
        base = pl.multiple_of(b * rows, 16)
        h0, h1 = slot_hits(slot_ref, base, rows)
        pick = jnp.where(h0 | h1, 1.0, 0.0).astype(BF16)
        tok_ref[pl.ds(base, rows), :] = dot(pick, sent[...]).astype(BF16)


def gelu_both(v):
    phi = 0.5 * (1.0 + lax.erf(v * 0.7071067811865476))
    slope = phi + v * jnp.exp(-0.5 * v * v) * 0.3989422804014327
    return v * phi, slope


def expert_kernel(
    fstep, srcs, cap,
    x_ref, og_ref, rw_ref, up_hbm, down_hbm,
    ret_ref, gs_ref, h_ref, gi_ref, gr_ref, gg_ref,
    up, down, acc, gacc, ggc, sem_up, sem_down,
):
    b = pl.program_id(0)

    @pl.when(b == 0)
    def _():
        load_blocks(up_hbm, up, sem_up)
        load_blocks(down_hbm, down, sem_down)
        ggc[...] = jnp.zeros_like(ggc)
        wait_all(up, sem_up)
        wait_all(down, sem_down)

    lane = lax.broadcasted_iota(jnp.int32, (1, 128), 1)
    experts = rw_ref.shape[1]
    x = x_ref[...]
    rw_hi, rw_lo = split_bf16(rw_ref[...])
    logits = dot(x, rw_hi) + dot(x, rw_lo)
    e = jnp.exp(logits - jnp.max(logits, axis=1, keepdims=True))
    own = lax.broadcasted_iota(jnp.int32, (1, experts), 1) == lax.axis_index("row")
    w = jnp.sum(jnp.where(own, e, 0.0), axis=1, keepdims=True) / jnp.sum(e, axis=1, keepdims=True)
    gr_ref[...] = (og_ref[...].astype(F32) * w).astype(BF16)
    acc[...] = jnp.zeros_like(acc)
    gacc[...] = jnp.zeros_like(gacc)

    @pl.loop(0, up.shape[1] // fstep)
    def _(f):
        cols = pl.ds(pl.multiple_of(f * fstep, fstep), fstep)
        inner = dot(x_ref[...], up[:, cols])
        hid, slope = gelu_both(inner)
        hid = hid.astype(BF16)
        h_ref[:, cols] = hid
        gh = dot_nt(gr_ref[...], down[cols, :])
        gi = (gh * slope).astype(BF16)
        gi_ref[:, cols] = gi
        acc[...] += dot(hid, down[cols, :])
        gacc[...] += dot_nt(gi, up[:, cols])

    gs_ref[...] = gacc[...].astype(BF16)
    ret = acc[...]
    ret_ref[...] = (w * ret).astype(BF16)
    gg = jnp.sum(ret.astype(BF16).astype(F32) * og_ref[...].astype(F32), axis=1, keepdims=True)
    old = ggc[0:cap, :]
    for s in range(srcs):
        old = jnp.where(lane == b * srcs + s, gg[s * cap : (s + 1) * cap], old)
    ggc[0:cap, :] = old

    @pl.when(b == pl.num_programs(0) - 1)
    def _():
        gg_ref[...] = jnp.transpose(ggc[...])[0 : gg_ref.shape[0], :]


def weight_grad_kernel(x_ref, gr_ref, h_ref, gi_ref, up_ref, down_ref, xt):
    @pl.when(pl.program_id(0) == 0)
    def _():
        xt[...] = jnp.transpose(x_ref[...])

    up = dot(xt[...], gi_ref[...]).astype(BF16)
    half = up_ref.shape[1]
    for c in range(up_ref.shape[0]):
        up_ref[c, :, :] = up[c * half : (c + 1) * half, :]
    down = dot_tn(h_ref[...], gr_ref[...]).astype(BF16)
    wide = down_ref.shape[2]
    for c in range(down_ref.shape[0]):
        down_ref[c, :, :] = down[:, c * wide : (c + 1) * wide]


def build_combine(slotc_ref, comb):
    padded, slots = comb.shape
    s0 = jnp.broadcast_to(slotc_ref[:, 0:1], (padded, 128))
    s1 = jnp.broadcast_to(slotc_ref[:, 1:2], (padded, 128))
    at = lax.broadcasted_iota(jnp.int32, (padded, 128), 1)

    @pl.loop(0, slots // 128)
    def _(j):
        here = at + j * 128
        cols = pl.ds(pl.multiple_of(j * 128, 128), 128)
        comb[:, cols] = jnp.where((s0 == here) | (s1 == here), 1.0, 0.0).astype(BF16)


def backward_kernel(
    images, experts,
    x_ref, og_ref, wt_ref, g1_ref, g2_ref, rw_ref, slot_ref, slotc_ref,
    proj_ref, mixed_ref, lse_ref, res_ref, probs_ref, gback_ref, gg_ref,
    xgrad_ref, wgrad_ref, rgrad_ref, gains_ref,
    xs, ogs, comb, big, gres, gb, gmix, gproj, n1, glt, gcol, gacc,
):
    padded, width = xs.shape
    pad_rows(x_ref, xs)
    pad_rows(og_ref, ogs)
    cap = gback_ref.shape[0] // experts
    build_combine(slotc_ref, comb)

    gcol[...] = jnp.zeros_like(gcol)
    gcol[0:experts, :] = gg_ref[...]
    gt = jnp.transpose(gcol[...])[0:cap]
    expert_at = lax.broadcasted_iota(jnp.int32, (experts, padded), 0)
    held = jnp.zeros((experts, padded), F32)
    for e in range(experts):
        h0, h1 = slot_hits(slot_ref, e * cap, cap)
        row = jnp.sum(jnp.where(h0 | h1, gt[:, e : e + 1], 0.0), axis=0, keepdims=True)
        held = jnp.where(expert_at == e, row, held)
    probs = probs_ref[...]
    gl = probs * (held - jnp.sum(probs * held, axis=0, keepdims=True))
    gl_hi, gl_lo = split_bf16(gl)
    rw_hi, rw_lo = split_bf16(rw_ref[...])
    glt[...] = jnp.concatenate([gl_hi, gl_lo, gl_hi], axis=0)
    rw3 = jnp.concatenate([rw_hi, rw_hi, rw_lo], axis=0)

    @pl.loop(0, width // 256)
    def _(j):
        cols = pl.ds(pl.multiple_of(j * 256, 256), 256)
        big[:, cols] = dot(comb[...], gback_ref[:, cols])

    for j in range(width // 256):
        cols = slice(j * 256, (j + 1) * 256)
        big[:, cols] = big[:, cols] + dot_tn(glt[...], rw3[:, cols])

    gacc[...] = jnp.zeros_like(gacc)

    def norm_two(rows):
        n, r = norm_parts(res_ref[rows, :])
        g = big[rows, :]
        u = g * g2_ref[...]
        back = r * (
            u - jnp.mean(u, axis=-1, keepdims=True) - n * jnp.mean(u * n, axis=-1, keepdims=True)
        )
        total = ogs[rows, :].astype(F32) + back
        gres[rows, :] = total
        gb[rows, :] = total.astype(BF16)
        n1[rows, :] = (n * g2_ref[...]).astype(BF16)
        gacc[0:8, :] += jnp.sum((g * n).reshape(-1, 8, width), axis=0)

    row_loop(padded, 32, norm_two)
    both = dot(jnp.concatenate([gl_hi, gl_lo], axis=0), n1[...])
    rgrad_ref[...] = both[:experts] + both[experts:]
    nc = wt_ref.shape[0]
    cw, ow = 3 * width // nc, width // nc
    for c in range(nc):
        wgrad_ref[c, :, cw:] = dot_tn(mixed_ref[...], gb[:, c * ow : (c + 1) * ow]).astype(BF16)
    gmix[...] = sum(
        dot_nt(gb[:, c * ow : (c + 1) * ow], wt_ref[c, :, cw:]) for c in range(nc)
    ).astype(BF16)

    def norm_one(rows):
        n, _ = norm_parts(xs[rows, :].astype(F32))
        n1[rows, :] = (n * g1_ref[...]).astype(BF16)

    row_loop(padded, 32, norm_one)
    gproj[...] = jnp.zeros_like(gproj)
    lane = lax.broadcasted_iota(jnp.int32, (1, 128), 1)
    first = lane < HEAD_DIM
    key_at = lax.broadcasted_iota(jnp.int32, (1, WIN), 1)
    row_at = lax.broadcasted_iota(jnp.int32, (WIN, 1), 0)

    def stack(v):
        return jnp.concatenate([jnp.where(first, v, 0.0), jnp.where(first, 0.0, v)], axis=0).astype(BF16)

    @pl.loop(0, HEADS // 2)
    def _(p):
        qc = pl.ds(pl.multiple_of(p * 128, 128), 128)
        kc = pl.ds(pl.multiple_of(width + p * 128, 128), 128)
        vc = pl.ds(pl.multiple_of(2 * width + p * 128, 128), 128)
        for i in range(images):
            rows = slice(STEP * i, STEP * i + WIN)
            off = (SEQ - STEP) * i
            bias = jnp.where((key_at >= off) & (key_at < off + SEQ), 0.0, NEG)
            valid = (row_at >= off) & (row_at < off + SEQ)
            qq = stack(proj_ref[rows, qc].astype(F32) * 0.125)
            k = proj_ref[rows, kc]
            v = proj_ref[rows, vc]
            gg = stack(gmix[rows, qc].astype(F32))
            ls = lse_ref[rows, :]
            l0 = jnp.sum(jnp.where(lane == 2 * p, ls, 0.0), axis=1, keepdims=True)
            l1 = jnp.sum(jnp.where(lane == 2 * p + 1, ls, 0.0), axis=1, keepdims=True)
            lse = jnp.concatenate([jnp.where(valid, l0, -NEG), jnp.where(valid, l1, -NEG)], axis=0)
            pr = jnp.exp(dot_nt(qq, k) + bias - lse)
            gp = dot_nt(gg, v)
            delta = jnp.sum(pr * gp, axis=1, keepdims=True)
            gs = (pr * (gp - delta)).astype(BF16)
            gq2 = dot(gs, k)
            gq = jnp.where(first, gq2[:WIN], gq2[WIN:]) * 0.125
            gk = dot_tn(gs, qq)
            gv = dot_tn(pr.astype(BF16), gg)
            for cols, val in ((qc, gq), (kc, gk), (vc, gv)):
                old = gproj[rows, cols].astype(F32)
                gproj[rows, cols] = jnp.where(valid, val, old).astype(BF16)

    for c in range(nc):
        cols = slice(c * cw, (c + 1) * cw)
        wgrad_ref[c, :, 0:cw] = dot_tn(n1[...], gproj[:, cols]).astype(BF16)
    big[...] = sum(
        dot_nt(gproj[:, c * cw : (c + 1) * cw], wt_ref[c, :, 0:cw]) for c in range(nc)
    )
    gacc[8:16, :] = jnp.zeros((8, width), F32)

    def norm_one_back(rows):
        n, r = norm_parts(xs[rows, :].astype(F32))
        g = big[rows, :]
        u = g * g1_ref[...]
        back = r * (
            u - jnp.mean(u, axis=-1, keepdims=True) - n * jnp.mean(u * n, axis=-1, keepdims=True)
        )
        gb[rows, :] = (gres[rows, :] + back).astype(BF16)
        gacc[8:16, :] += jnp.sum((g * n).reshape(-1, 8, width), axis=0)

    row_loop(padded, 32, norm_one_back)
    xgrad_ref[...] = gb[0 : xgrad_ref.shape[0], :]
    gains_ref[...] = jnp.concatenate(
        [
            jnp.sum(gacc[8:16, :], axis=0, keepdims=True),
            jnp.sum(gacc[0:8, :], axis=0, keepdims=True),
        ],
        axis=0,
    )


def combine_kernel(slotc_ref, res_ref, back_ref, out_ref, sq_ref, comb, acc):
    build_combine(slotc_ref, comb)

    @pl.loop(0, acc.shape[1] // 256)
    def _(j):
        cols = pl.ds(pl.multiple_of(j * 256, 256), 256)
        branch = dot(comb[...], back_ref[:, cols])
        result = res_ref[:, cols] + branch
        acc[:, cols] = result.astype(BF16)
        sq_ref[0:1, cols] = jnp.sum(result * result, axis=0, keepdims=True)
        sq_ref[1:2, cols] = jnp.sum(branch * branch, axis=0, keepdims=True)

    out_ref[...] = acc[0 : out_ref.shape[0], :]


def shape(dims, dtype=BF16):
    return jax.ShapeDtypeStruct(dims, dtype)


def per_device(
    block_input, attention_in, attention_out, expert_up, expert_down, router_weight,
    gain_attention, gain_experts, expert_ids, expert_slots, expert_capacity, keep_mask, output_grad,
):
    tokens, width = block_input.shape
    images = tokens // SEQ
    padded = STEP * images + (WIN - STEP)
    experts = expert_capacity.shape[0]
    cap = (2 * tokens * 11 // (8 * experts) + 7) // 8 * 8
    slots = experts * cap
    cap_lanes = cdiv(cap, 128) * 128
    nrow, ncol = lax.axis_size("row"), lax.axis_size("col")
    ff = expert_up.shape[2]
    blocks = 4
    aligned = (width // ncol) % 128 == 0

    ring = nrow == 16 and ncol == 2
    own_weights = jnp.concatenate([attention_in, attention_out], axis=1)
    rh, wcols = own_weights.shape
    if ring:
        weights = pl.pallas_call(
            gather_kernel,
            out_shape=shape((ncol, width, wcols)),
            in_specs=[VMEM],
            out_specs=VMEM,
            scratch_shapes=[DMA((3,)), DMA((3,)), DMA((8,)), DMA((8,)), DMA((8,)), DMA((8,)),
                            DMA((16,)), DMA((16,)), DMA],
            compiler_params=params(24, collective_id=0, has_side_effects=True),
            name="attn_weights_gather",
        )(own_weights)
    else:
        weights = jnp.concatenate(
            [
                lax.all_gather(lax.all_gather(v, "col", axis=1, tiled=True), "row", axis=0, tiled=True)
                for v in (attention_in, attention_out)
            ],
            axis=1,
        )[None]
    if aligned:
        up_blocks = lax.all_gather(expert_up[0], "col", axis=0, tiled=False)
        down_blocks = lax.all_gather(expert_down[0], "col", axis=0, tiled=False)
    else:
        up_blocks = lax.all_gather(expert_up, "col", axis=1, tiled=True)
        down_blocks = lax.all_gather(expert_down, "col", axis=2, tiled=True)

    limit = jnp.sum(
        jnp.where(
            expert_ids[:, :, None] == jnp.arange(experts, dtype=jnp.int32)[None, None, :],
            expert_capacity[None, None, :],
            0,
        ),
        axis=-1,
    )
    used = (keep_mask == 1) & (expert_slots < limit)
    slot_index = jnp.where(used, expert_ids * cap + expert_slots, -1)
    slot_cols = jnp.pad(slot_index, ((0, padded - tokens), (0, 0)), constant_values=-1)
    slot_rows = slot_cols.T
    g1 = gain_attention.reshape(1, width)
    g2 = gain_experts.reshape(1, width)
    rwt = router_weight.T

    og_out = pl.pallas_call(
        functools.partial(dispatch_kernel, blocks),
        out_shape=shape((slots, width)),
        in_specs=[VMEM, VMEM],
        out_specs=VMEM,
        scratch_shapes=[pltpu.VMEM((padded, width), BF16)],
        compiler_params=params(24),
        name="og_dispatch",
    )(output_grad, slot_rows)

    def exchange(v):
        return lax.all_to_all(v, "row", split_axis=0, concat_axis=0, tiled=True)

    og_in = exchange(og_out.reshape(experts, cap, width)).reshape(slots, width)

    proj, mixed, lse, res, probs, tok_out, sq_attn = pl.pallas_call(
        functools.partial(forward_kernel, images, experts, blocks),
        out_shape=[
            shape((padded, 3 * width)),
            shape((padded, width)),
            shape((padded, 128), F32),
            shape((padded, width), F32),
            shape((experts, padded), F32),
            shape((slots, width)),
            shape((1, width), F32),
        ],
        in_specs=[VMEM] * 6,
        out_specs=[VMEM] * 7,
        scratch_shapes=[pltpu.VMEM((padded, width), BF16)] * 4,
        compiler_params=params(48),
        cost_estimate=pl.CostEstimate(flops=6 * 10**9, bytes_accessed=90 * 10**6, transcendentals=0),
        name="attn_forward",
    )(block_input, weights, g1, g2, rwt, slot_rows)

    tok_in = exchange(tok_out.reshape(experts, cap, width)).reshape(slots, width)

    rblk = slots // blocks
    whole = lambda *dims: pl.BlockSpec(dims, lambda b: (0,) * len(dims))
    rows_spec = lambda n: pl.BlockSpec((rblk, n), lambda b: (b, 0))
    ret, gsent, hid, ginner, gr, gg_out = pl.pallas_call(
        functools.partial(expert_kernel, 512, experts // blocks, cap),
        grid=(blocks,),
        out_shape=[
            shape((slots, width)),
            shape((slots, width)),
            shape((slots, ff)),
            shape((slots, ff)),
            shape((slots, width)),
            shape((experts, cap_lanes), F32),
        ],
        in_specs=[rows_spec(width), rows_spec(width), whole(width, experts), ANY, ANY],
        out_specs=[
            rows_spec(width), rows_spec(width), rows_spec(ff), rows_spec(ff), rows_spec(width),
            whole(experts, cap_lanes),
        ],
        scratch_shapes=[
            pltpu.VMEM((width, ff), BF16),
            pltpu.VMEM((ff, width), BF16),
            pltpu.VMEM((rblk, width), F32),
            pltpu.VMEM((rblk, width), F32),
            pltpu.VMEM((cap_lanes, 128), F32),
            DMA,
            DMA,
        ],
        compiler_params=params(56),
        cost_estimate=pl.CostEstimate(flops=4 * 10**10, bytes_accessed=150 * 10**6, transcendentals=0),
        name="expert_fused",
    )(tok_in, og_in, router_weight, up_blocks, down_blocks)

    gg_all = lax.all_gather(gg_out, "row", axis=0, tiled=False)
    gg_back = lax.dynamic_index_in_dim(gg_all, lax.axis_index("row"), 1, keepdims=False)
    gback = exchange(gsent.reshape(experts, cap, width)).reshape(slots, width)
    ret, _ = lax.optimization_barrier((ret, gsent))
    back = exchange(ret.reshape(experts, cap, width)).reshape(slots, width)

    fstep = 512
    nc = ncol if aligned else 1
    up_part, down_part = pl.pallas_call(
        weight_grad_kernel,
        grid=(ff // fstep,),
        out_shape=[shape((nc, width // nc, ff)), shape((nc, ff, width // nc))],
        in_specs=[
            whole(slots, width),
            whole(slots, width),
            pl.BlockSpec((slots, fstep), lambda f: (0, f)),
            pl.BlockSpec((slots, fstep), lambda f: (0, f)),
        ],
        out_specs=[
            pl.BlockSpec((nc, width // nc, fstep), lambda f: (0, 0, f)),
            pl.BlockSpec((nc, fstep, width // nc), lambda f: (0, f, 0)),
        ],
        scratch_shapes=[pltpu.VMEM((width, slots), BF16)],
        compiler_params=params(56),
        cost_estimate=pl.CostEstimate(flops=2 * 10**10, bytes_accessed=80 * 10**6, transcendentals=0),
        name="expert_weight_grads",
    )(tok_in, gr, hid, ginner)
    if aligned:
        up_grad = lax.psum_scatter(up_part, "col", scatter_dimension=0, tiled=True).astype(F32)
        down_grad = lax.psum_scatter(down_part, "col", scatter_dimension=0, tiled=True).astype(F32)
    else:
        up_grad = lax.psum_scatter(up_part, "col", scatter_dimension=1, tiled=True).astype(F32)
        down_grad = lax.psum_scatter(down_part, "col", scatter_dimension=2, tiled=True).astype(F32)

    x_grad, wgrad, rgrad, gains = pl.pallas_call(
        functools.partial(backward_kernel, images, experts),
        out_shape=[
            shape((tokens, width)),
            shape(weights.shape),
            shape((experts, width), F32),
            shape((2, width), F32),
        ],
        in_specs=[VMEM] * 15,
        out_specs=[VMEM] * 4,
        scratch_shapes=[
            pltpu.VMEM((padded, width), BF16),
            pltpu.VMEM((padded, width), BF16),
            pltpu.VMEM((padded, slots), BF16),
            pltpu.VMEM((padded, width), F32),
            pltpu.VMEM((padded, width), F32),
            pltpu.VMEM((padded, width), BF16),
            pltpu.VMEM((padded, width), BF16),
            pltpu.VMEM((padded, 3 * width), BF16),
            pltpu.VMEM((padded, width), BF16),
            pltpu.VMEM((3 * experts, padded), BF16),
            pltpu.VMEM((128, cap_lanes), F32),
            pltpu.VMEM((16, width), F32),
        ],
        compiler_params=params(58),
        cost_estimate=pl.CostEstimate(flops=2 * 10**10, bytes_accessed=180 * 10**6, transcendentals=0),
        name="attn_backward",
    )(
        block_input, output_grad, weights, g1, g2, rwt, slot_rows, slot_cols,
        proj, mixed, lse, res, probs, gback, gg_back,
    )
    block_output, sq_moe = pl.pallas_call(
        combine_kernel,
        out_shape=[shape((tokens, width)), shape((2, width), F32)],
        in_specs=[VMEM] * 3,
        out_specs=[VMEM] * 2,
        scratch_shapes=[pltpu.VMEM((padded, slots), BF16), pltpu.VMEM((padded, width), BF16)],
        compiler_params=params(32),
        cost_estimate=pl.CostEstimate(flops=3 * 10**9, bytes_accessed=16 * 10**6, transcendentals=0),
        name="moe_combine",
    )(slot_cols, res, back)

    small = jnp.concatenate([rgrad, gains, sq_moe, sq_attn], axis=0)
    small = jnp.pad(small, ((0, -small.shape[0] % 8), (0, 0)))
    if ring:
        half = wcols // 2
        blk = lambda *lead: pltpu.VMEM(lead + (rh, wcols), BF16)
        hblk = lambda *lead: pltpu.VMEM(lead + (rh, half), BF16)
        merged, small = pl.pallas_call(
            reduce_kernel,
            out_shape=[shape((rh, wcols), F32), shape(small.shape, F32)],
            in_specs=[VMEM] * 2,
            out_specs=[VMEM] * 2,
            scratch_shapes=[
                blk(4, 2, 2), blk(4, 2, 2), hblk(4, 2), hblk(4, 2), hblk(4), hblk(4), blk(3),
                pltpu.VMEM((5,) + small.shape, F32), pltpu.VMEM((5,) + small.shape, F32),
                DMA((16,)), DMA((16,)), DMA((8,)), DMA((8,)), DMA((8,)), DMA((8,)),
                DMA((3,)), DMA((3,)), DMA((5,)), DMA((5,)),
            ],
            compiler_params=params(40, collective_id=1, has_side_effects=True),
            name="attn_grads_reduce",
        )(wgrad, small)
        in_grad = merged[:, : 3 * width // ncol]
        out_grad = merged[:, 3 * width // ncol :]
    else:
        merged = lax.psum_scatter(wgrad[0], "row", scatter_dimension=0, tiled=True)
        in_grad = lax.psum_scatter(
            merged[:, : 3 * width], "col", scatter_dimension=1, tiled=True
        ).astype(F32)
        out_grad = lax.psum_scatter(
            merged[:, 3 * width :], "col", scatter_dimension=1, tiled=True
        ).astype(F32)
        small = lax.psum(small, ("row", "col"))
    rgrad = small[:experts]
    gains = small[experts : experts + 2]
    sums = jnp.sum(small[experts + 2 : experts + 5], axis=1)
    squares = jnp.stack([sums[0], sums[2], sums[1]])
    residual_rms = jnp.sqrt(squares / (tokens * nrow * ncol * width))
    return (
        block_output, x_grad, in_grad, out_grad,
        up_grad.reshape(1, width // ncol, ff), down_grad.reshape(1, ff, width // ncol),
        rgrad.T, gains[0], gains[1], residual_rms,
    )


def solution(mesh):
    tok = P(("row", "col"), None)
    grid = P("row", "col")
    up, down = P("row", "col", None), P("row", None, "col")
    return jax.shard_map(
        per_device,
        mesh=mesh,
        in_specs=(tok, grid, grid, up, down, P(), P(), P(), tok, tok, P(), tok, tok),
        out_specs=(tok, tok, grid, grid, up, down, P(), P(), P(), P()),
        check_vma=False,
    )
```

time: 848 us -> 638 us (0.75); the launches traced: 836 us -> 637 us
  Pallas kernels: 0 us -> 284 us
  local copies, waits for them, and re-layouts: 214 us -> 18.7 us
  matrix products: 191 us -> 0 us
  other arithmetic: 81.6 us -> 14.4 us
  waiting for transfers between devices: 228 us -> 184 us
  blocking collectives: 55.4 us -> 72.1 us
    pallas_call x0 -> x8, Pallas kernels: none -> 284 us  [the longest x1 64.7 us: per_device(): pl.pallas_call(functools.partial(expert_kernel, 512, experts // blocks, c...]
    dot_general x21 -> x0, matrix products: 191 us -> none  [the longest x1 26.1 us: per_device(): jnp.einsum('rlcd,lfd->rlcf', grad_arrived, down_full, preferred_element_t...]
    unnamed x137 -> x43, local copies, waits for them, and re-layouts: 77 us -> 14 us
    reduce_scatter x3 -> x2, waiting for transfers between devices: 61 us -> 0.01 us  [the longest x1 0.01 us: per_device(): lax.psum_scatter(up_part, 'col', scatter_dimension=0, tiled=True)]
    all_gather x2 -> x1, blocking collectives: 13.6 us -> 72.1 us  [per_device(): gg_all = lax.all_gather(gg_out, 'row', axis=0, tiled=False)]
    gather x11 -> x0, local copies, waits for them, and re-layouts: 49.4 us -> none  [the longest x7 21 us: route_gates(): return jnp.take_along_axis(router_probs, expert_ids, axis=1)]
    all_to_all x4, waiting for transfers between devices: 73.3 us -> 118 us  [exchange(): return lax.all_to_all(v, 'row', split_axis=0, concat_axis=0, tiled=True)]
    psum x1 -> x0, blocking collectives: 41.9 us -> none  [per_device(): lax.psum((router_grad_part, gain_attention_part, gain_experts_part, squar...]
  transfers between devices with their start and end apart: 14 -> 8, of which waited for: 9 -> 3; matrix products, arithmetic and copies ran while one was open for 45% -> 2% of each run, Pallas kernels for 0% -> 20%
where the time goes in v1:
time: 638 us; the launch traced here: 637 us
  Pallas kernels  284 us (45%)
  waiting for transfers between devices  184 us (29%)
  blocking collectives  72.1 us (11%)
  starting transfers between devices  50.3 us (8%)
  local copies, waits for them, and re-layouts  18.7 us (3%)
  other arithmetic  14.4 us (2%)
  between operations  14 us (2%)
    all_to_all x4, waiting for transfers between devices, exchange(): return lax.all_to_all(v, 'row', split_axis=0, concat_axis=0, tiled=True)  118 us
    all_gather x1, blocking collectives, per_device(): gg_all = lax.all_gather(gg_out, 'row', axis=0, tiled=False)  72.1 us
    pallas_call x1, Pallas kernels, per_device(): pl.pallas_call(functools.partial(expert_kernel, 512, experts // blocks, c...  64.7 us
    all_gather x1, waiting for transfers between devices, per_device(): down_blocks = lax.all_gather(expert_down[0], 'col', axis=0, tiled=False)  64.2 us
    pallas_call x1, Pallas kernels, per_device(): pl.pallas_call(functools.partial(backward_kernel, images, experts), out_s...  60.5 us
    pallas_call x1, Pallas kernels, per_device(): pl.pallas_call(reduce_kernel, out_shape=[shape((rh, wcols), F32), shape(s...  54 us
    all_to_all x4, starting transfers between devices, exchange(): return lax.all_to_all(v, 'row', split_axis=0, concat_axis=0, tiled=True)  50 us
    pallas_call x1, Pallas kernels, per_device(): pl.pallas_call(gather_kernel, out_shape=shape((ncol, width, wcols)), in_s...  32.2 us
  transfers between devices with their start and end apart: 8, of which 3 were waited for; matrix products, arithmetic and copies ran while one was open for 2% of the time, Pallas kernels for 20%

profile of v1, /device:TPU:0, one launch (start us, length us, event | category | flops | bytes accessed | tf_op | source)
XLA Modules:
  0.0 637.5 jit_solution(2883492517852805220)
XLA Ops:
  12.0 32.2 %attn_weights_gather.1.wt_ref = bf16[2,768,1536]{2,1,0:T(8,128)(2,1)S(1)} custom-call(bf16[48,1536]{1,0:T(8,128)(2,1)S(1)} %pad_maximum_fusion.own_ref), custom_call_target="tpu_custom_call" | custom-call | tf_op jit(solution)/shard_map/attn_weights_gather/pallas_call | solution.py:632
  44.1 2.2 copy-done
  46.5 31.0 %attn_forward.1 = (bf16[800,2304]{1,0:T(8,128)(2,1)}, bf16[800,768]{1,0:T(8,128)(2,1)S(1)}, f32[800,128]{1,0:T(8,128)S(1)}, f32[800,768]{1,0:T(8,128)S(1)}, f32[...) custom-call(bf16[788,768]{1,0:T(8,128)(2,1)S(1)} %copy-done.8, bf16[2,768,1536]{2,1,0:T(8,128)(2,1)} %copy-done, ...), custom_call_target="tpu_custom_call" | custom-call | flops 6000000000 | bytes 90000000 | tf_op jit(solution)/shard_map/attn_forward/pallas_call | solution.py:688
  77.6 1.4 copy-done.9
  80.2 4.5 all-to-all-start
  85.4 6.2 og_dispatch.1
  91.6 55.8 %all-to-all-done = bf16[16,136,768]{2,1,0:T(8,128)(2,1)} async-done(((bf16[16,136,768]{2,1,0:T(8,128)(2,1)}), bf16[16,136,768]{2,1,0:T(8,128)(2,1)}, u32[]{:S(2)}, u32[]{:S(2)}) %all-to-all-start) | async-done | bytes 3342368 | tf_op jit(solution)/shard_map/all_to_all | solution.py:684
  147.4 16.2 %all-to-all-start.1 = ((bf16[16,136,768]{2,1,0:T(8,128)(2,1)}), bf16[16,136,768]{2,1,0:T(8,128)(2,1)S(1)}, u32[]{:S(2)}, u32[]{:S(2)}) async-start(bf16[16,136,768]{2,1,0:T(8,128)(2,1)} %bitcast.4), calls=%async_computation.1 | async-start | bytes 6684672 | tf_op jit(solution)/shard_map/all_to_all | solution.py:684
  165.5 64.2 %all-gather.6.cloned.1.call-done.down_hbm = bf16[2,3072,384]{2,1,0:T(8,128)(2,1)} async-done(((bf16[1,3072,384]{2,1,0:T(8,128)(2,1)}), bf16[2,3072,384]{2,1,0:T(8,128)(2,1)}) %all-gather.6.cloned.1.call-update) | async-done | bytes 4718608 | tf_op jit(solution)/shard_map/all_gather | solution.py:652
  229.8 1.7 copy-done.14
  231.5 64.7 %expert_fused.1 = (bf16[2176,768]{1,0:T(8,128)(2,1)}, bf16[2176,768]{1,0:T(8,128)(2,1)}, bf16[2176,3072]{1,0:T(8,128)(2,1)}, bf16[2176,3072]{1,0:T(8,128)(2,1)},...) custom-call(bf16[2176,768]{1,0:T(8,128)(2,1)} %bitcast.3.x_ref, bf16[2176,768]{1,0:T(8,128)(2,1)} %bitcast.22, ...), custom_call_target="tpu_custom_call" | custom-call | flops 40000000000 | bytes 150000000 | tf_op jit(solution)/shard_map/expert_fused/pallas_call | solution.py:712
  296.2 29.2 %expert_weight_grads.1 = (bf16[2,384,3072]{2,1,0:T(8,128)(2,1)}, bf16[2,3072,384]{2,1,0:T(8,128)(2,1)}) custom-call(bf16[2176,768]{1,0:T(8,128)(2,1)} %bitcast.3.x_ref, bf16[2176,768]{1,0:T(8,128)(2,1)} %get-tuple-element.52.gr_ref, bf16[2176,3072]{1,0:T(8,128)(2,1)} %get-tuple-element.53.h_ref, bf16[2176,3072]{1,0:T(8,128)(2,1)} %get-tuple-element.54.gi_ref), custom_call_target="tpu_custom_call" | custom-call | flops 20000000000 | bytes 80000000 | tf_op jit(solution)/shard_map/expert_weight_grads/pallas_call | solution.py:750
  325.4 12.9 %all-to-all-start.2 = ((bf16[16,136,768]{2,1,0:T(8,128)(2,1)}), bf16[16,136,768]{2,1,0:T(8,128)(2,1)S(1)}, u32[]{:S(2)}, u32[]{:S(2)}) async-start(bf16[16,136,768]{2,1,0:T(8,128)(2,1)} %bitcast.21), calls=%async_computation.2 | async-start | bytes 6684672 | tf_op jit(solution)/shard_map/all_to_all | solution.py:684
  338.9 62.2 %all-to-all-done.2 = bf16[16,136,768]{2,1,0:T(8,128)(2,1)S(1)} async-done(((bf16[16,136,768]{2,1,0:T(8,128)(2,1)}), bf16[16,136,768]{2,1,0:T(8,128)(2,1)S(1)}, u32[]{:S(2)}, u32[]{:S(2)}) %all-to-all-start.2) | async-done | bytes 3342368 | tf_op jit(solution)/shard_map/all_to_all | solution.py:684
  401.1 16.4 %all-to-all-start.3 = ((bf16[16,136,768]{2,1,0:T(8,128)(2,1)}), bf16[16,136,768]{2,1,0:T(8,128)(2,1)}, u32[]{:S(2)}, u32[]{:S(2)}) async-start(bf16[16,136,768]{2,1,0:T(8,128)(2,1)} %bitcast.20), calls=%async_computation.3 | async-start | bytes 6684672 | tf_op jit(solution)/shard_map/all_to_all | solution.py:684
  417.5 72.1 %all-gather = f32[256,256]{1,0:T(8,128)S(1)} all-gather(f32[16,256]{1,0:T(8,128)S(1)} %copy-done.17), channel_id=2, replica_groups=mesh['row'=16,'col'=2] {'row'}, dimensions={0}, use_global_device_ids=true | all-gather | bytes 278528 | tf_op jit(solution)/shard_map/all_gather | solution.py:742
  491.3 1.7 copy-done.10
  493.0 5.9 moe_combine.1
  498.9 60.5 %attn_backward.1 = (bf16[788,768]{1,0:T(8,128)(2,1)}, bf16[2,768,1536]{2,1,0:T(8,128)(2,1)}, f32[16,768]{1,0:T(8,128)}, f32[2,768]{1,0:T(2,128)}) custom-call(bf16[788,768]{1,0:T(8,128)(2,1)} %x_ref.3, bf16[788,768]{1,0:T(8,128)(2,1)} %og_ref.1, bf16[2,768,1536]{2,1,0:T(8,128)(2,1)} %copy-done, f32[1,768]{1,0:T(1,128)} %copy-done.6, f32[1,768]{1,0:T(1,128)} %copy-done.7, ...), custom_call_target="tpu_custom_call" | custom-call | flops 20000000000 | bytes 180000000 | tf_op jit(solution)/shard_map/attn_backward/pallas_call | solution.py:776
  560.3 2.3 copy-done.1
  562.6 54.0 %attn_grads_reduce.1 = (f32[48,1536]{1,0:T(8,128)S(1)}, f32[24,768]{1,0:T(8,128)S(1)}) custom-call(bf16[2,768,1536]{2,1,0:T(8,128)(2,1)S(1)} %copy-done.1, f32[24,768]{1,0:T(8,128)S(1)} %select_maximum_fusion.small_ref), custom_call_target="tpu_custom_call" | custom-call | tf_op jit(solution)/shard_map/attn_grads_reduce/pallas_call | solution.py:824
  618.6 2.5 fusion
  622.4 4.4 convert_element_type.8
  626.8 4.2 convert_element_type.9
  (71 shorter events, 15.0 us)
Async XLA Ops:
  7.2 4.8 copy-start.16
  7.2 4.7 copy-start.15
  11.1 35.2 %copy-start.18 = (f32[768]{0:T(1024)S(1)}, f32[768]{0:T(1024)}, u32[]{:S(2)}) copy-start(f32[768]{0:T(1024)} %param.19) | copy-start | bytes 9220
  11.1 35.2 %copy-start.19 = (f32[768]{0:T(1024)S(1)}, f32[768]{0:T(1024)}, u32[]{:S(2)}) copy-start(f32[768]{0:T(1024)} %param.20) | copy-start | bytes 9220
  11.1 35.4 %copy-start.4 = (f32[768,16]{0,1:T(8,128)S(1)}, f32[768,16]{0,1:T(8,128)}, u32[]{:S(2)}) copy-start(f32[768,16]{0,1:T(8,128)} %param.18) | copy-start | bytes 147460
  11.1 35.4 %copy-start.8 = (bf16[788,768]{1,0:T(8,128)(2,1)S(1)}, bf16[788,768]{1,0:T(8,128)(2,1)}, u32[]{:S(2)}) copy-start(bf16[788,768]{1,0:T(8,128)(2,1)} %x_ref.3) | copy-start | bytes 3631108
  44.1 2.2 copy-start
  46.3 31.3 %copy-start.6 = (f32[1,768]{1,0:T(1,128)}, f32[1,768]{1,0:T(1,128)S(1)}, u32[]{:S(2)}) copy-start(f32[1,768]{1,0:T(1,128)S(1)} %reshape.52.g1_ref) | copy-start | bytes 9220
  46.3 31.2 %copy-start.7 = (f32[1,768]{1,0:T(1,128)}, f32[1,768]{1,0:T(1,128)S(1)}, u32[]{:S(2)}) copy-start(f32[1,768]{1,0:T(1,128)S(1)} %reshape.53.g2_ref) | copy-start | bytes 9220
  46.5 38.9 %copy-start.5 = (s32[2,800]{1,0:T(2,128)}, s32[2,800]{1,0:T(2,128)S(1)}, u32[]{:S(2)}) copy-start(s32[2,800]{1,0:T(2,128)S(1)} %copy.66.slot_ref) | copy-start | bytes 19204
  77.6 1.4 copy-start.9
  79.0 6.4 %copy-start.2 = (bf16[788,768]{1,0:T(8,128)(2,1)S(1)}, bf16[788,768]{1,0:T(8,128)(2,1)}, u32[]{:S(2)}) copy-start(bf16[788,768]{1,0:T(8,128)(2,1)} %og_ref.1) | copy-start | bytes 3631108
  80.2 67.3 %all-to-all-start = ((bf16[16,136,768]{2,1,0:T(8,128)(2,1)}), bf16[16,136,768]{2,1,0:T(8,128)(2,1)}, u32[]{:S(2)}, u32[]{:S(2)}) async-start(bf16[16,136,768]{2,1,0:T(8,128)(2,1)} %bitcast.23), calls=%async_computation | async-start | bytes 6684672 | tf_op jit(solution)/shard_map/all_to_all | solution.py:684
  84.7 80.9 %all-gather.4.cloned.1.call-start = ((), (), s32[]{:S(2)}) async-start(), calls=%async_computation.6 | async-start | bytes 7077888 | tf_op jit(solution)/shard_map/all_gather | solution.py:651
  147.4 82.3 %all-to-all-start.1 = ((bf16[16,136,768]{2,1,0:T(8,128)(2,1)}), bf16[16,136,768]{2,1,0:T(8,128)(2,1)S(1)}, u32[]{:S(2)}, u32[]{:S(2)}) async-start(bf16[16,136,768]{2,1,0:T(8,128)(2,1)} %bitcast.4), calls=%async_computation.1 | async-start | bytes 6684672 | tf_op jit(solution)/shard_map/all_to_all | solution.py:684
  163.6 66.1 %all-gather.6.cloned.1.call-start = ((), (), s32[]{:S(2)}) async-start(), calls=%async_computation.7 | async-start | bytes 7077888 | tf_op jit(solution)/shard_map/all_gather | solution.py:652
  164.4 458.0 %reduce-scatter.3.cloned.1.call-start = ((), (), s32[]{:S(2)}) async-start(), calls=%async_computation.8 | async-start | bytes 7077888 | tf_op jit(solution)/shard_map/reduce_scatter | solution.py:770
  229.7 1.7 copy-start.14
  325.4 75.7 %all-to-all-start.2 = ((bf16[16,136,768]{2,1,0:T(8,128)(2,1)}), bf16[16,136,768]{2,1,0:T(8,128)(2,1)S(1)}, u32[]{:S(2)}, u32[]{:S(2)}) async-start(bf16[16,136,768]{2,1,0:T(8,128)(2,1)} %bitcast.21), calls=%async_computation.2 | async-start | bytes 6684672 | tf_op jit(solution)/shard_map/all_to_all | solution.py:684
  338.3 288.5 %reduce-scatter.5.cloned.1.call-start = ((), (), s32[]{:S(2)}) async-start(), calls=%async_computation.9 | async-start | bytes 7077888 | tf_op jit(solution)/shard_map/reduce_scatter | solution.py:771
  401.1 16.4 %copy-start.17 = (f32[16,256]{1,0:T(8,128)S(1)}, f32[16,256]{1,0:T(8,128)}, u32[]{:S(2)}) copy-start(f32[16,256]{1,0:T(8,128)} %get-tuple-element.44) | copy-start | bytes 49156
  401.1 97.8 %all-to-all-start.3 = ((bf16[16,136,768]{2,1,0:T(8,128)(2,1)}), bf16[16,136,768]{2,1,0:T(8,128)(2,1)}, u32[]{:S(2)}, u32[]{:S(2)}) async-start(bf16[16,136,768]{2,1,0:T(8,128)(2,1)} %bitcast.20), calls=%async_computation.3 | async-start | bytes 6684672 | tf_op jit(solution)/shard_map/all_to_all | solution.py:684
  491.3 1.7 copy-start.10
  560.3 2.3 copy-start.1
  (4 other events, 4.4 us)
Sparse Core Ops, SparseCore 0:
  87.0 63.5 all-gather.3
  166.0 63.6 all-gather.5
  325.5 67.9 reduce-scatter.2
  395.8 59.9 reduce-scatter.4
